TPU v7x, 512 devices: a whole 4x4x16 slice. The times are simulated.
512 devices in a mesh: seq: 64 (over z, y), exp: 8 (over x, core).
Axes of the slice: x: 4, y: 4, z: 16, core: 2. Of those that a mesh axis runs over, the one named last changes fastest.
Arguments:
- x_in: bfloat16 [4096, 8192], P('seq', 'exp'), may hold values from -6 to 6
- z_gate: bfloat16 [4096, 8192], P('seq', 'exp'), may hold values from -6 to 6
- dt_low: bfloat16 [4096, 256], P('seq'), may hold values from -6 to 6
- dt_weight: bfloat16 [256, 8192], P(None, 'exp'), may hold values from -0.375 to 0.375
- dt_bias: float32 [8192], P('exp'), may hold values from -9 to -1
- a_log: float32 [16, 8192], P(None, 'exp'), may hold values from -4 to 0
- conv_weight: float32 [4, 8192], P(None, 'exp'), may hold values from -3 to 3
- conv_bias: float32 [8192], P('exp'), may hold values from -0.5 to 0.5
- d_skip: float32 [8192], P('exp'), may hold values from 0.5 to 1.5
- b_and_c: float32 [2, 16, 4096], P(None, None, 'seq'), may hold values from -6 to 6
- hidden: bfloat16 [4096, 4096], P('seq', 'exp'), may hold values from -6 to 6
- router: bfloat16 [4096, 8], P('exp'), may hold values from -0.09375 to 0.09375
- expert_ids: int32 [4096, 2], P('seq'), may hold values from 0 to 7, all different within a row; in each aligned block of 64 rows (0 to 63, 64 to 127, ...) at most 18 rows name the same one
- w_gate: bfloat16 [4096, 98304], P('exp', 'seq'), may hold values from -0.09375 to 0.09375
- w_down: bfloat16 [98304, 4096], P('seq', 'exp'), may hold values from -0.0546875 to 0.0546875
Outputs:
- mamba_out: bfloat16 [4096, 8192], P('seq', 'exp')
- moe_out: bfloat16 [4096, 4096], P('seq', 'exp')
Inputs may be any that keep to these rules, and one draw needn't show every extreme that they name: `expert_ids`: each token names 2 different experts; among the 64 tokens of one block no expert is named more than 18 times, a bound that some expert reaches in every block.
All inputs are finite; a program needn't handle non-finite values.
Results may differ from a plain program's by a relative error of at most 0.018.
Values may be sent and summed in bfloat16 or wider, within the bound.
A program may use at most 128 MiB of HBM per device.

v0:
```python
import jax
import jax.numpy as jnp
from jax import lax
from jax.sharding import PartitionSpec as P

CAP = 18


def passed_along(value, axis, steps):
    count = lax.axis_size(axis)
    first, last = (max(0, -steps), min(count, count - steps))
    return lax.ppermute(value, axis, [(source, source + steps) for source in range(first, last)])


def carried_in(array, axis, join, neutral):
    place = lax.axis_index(axis)
    gathered = jax.tree.map(
        lambda a, kind: lax.all_gather(a.astype(kind), axis), array, (jnp.bfloat16, jnp.bfloat16)
    )
    state = jax.tree.map(lambda a, e: jnp.zeros_like(a) + jnp.asarray(e, a.dtype), array, neutral)

    def one(lap, state):
        return join(
            state,
            jax.tree.map(
                lambda a, own: lax.dynamic_index_in_dim(a, lap, 0, False).astype(own.dtype),
                gathered,
                array,
            ),
        )

    return lax.fori_loop(0, place, one, state)


def link_pairs(earlier, later):
    return (earlier[0] * later[0], later[0] * earlier[1] + later[1])


def mixer_scan(delta, activated, b_rows, c_rows, rates, start_state):
    token_count, channels = delta.shape
    block_len = 16
    block_count = token_count // block_len

    def regroup(values):
        return values.reshape((block_count, block_len) + values.shape[1:])

    def advance(carry, inputs):
        running, product = carry
        step_delta, step_x, step_b, step_c = inputs
        reads = []
        for position in range(block_len):
            factor = jnp.exp(step_delta[position][None, :] * rates)
            running = (
                factor * running
                + step_b[position][:, None] * (step_delta[position] * step_x[position])[None, :]
            )
            product = factor * product
            reads.append(jnp.sum(step_c[position][:, None] * running, axis=0))
        return ((running, product), (jnp.stack(reads),))

    initial = (start_state, jnp.ones(rates.shape, jnp.float32))
    finals, outputs = lax.scan(
        advance, initial, (regroup(delta), regroup(activated), regroup(b_rows), regroup(c_rows))
    )
    readout = outputs[0].reshape(token_count, channels)
    weighted_all = None
    return (readout, weighted_all, finals[0], finals[1])


def local(
    x_in,
    z_gate,
    dt_low,
    dt_weight,
    dt_bias,
    a_log,
    conv_weight,
    conv_bias,
    d_skip,
    b_and_c,
    hidden,
    router,
    expert_ids,
    w_gate,
    w_down,
):
    tok_rows = x_in.shape[0]
    kernel_taps = conv_weight.shape[0]
    edge_rows = passed_along(x_in[tok_rows - (kernel_taps - 1) :], "seq", 1)
    padded = jnp.concatenate([edge_rows, x_in], axis=0).astype(jnp.float32)
    convolved = jnp.zeros(x_in.shape, jnp.float32) + conv_bias[None, :]
    for offset in range(kernel_taps):
        convolved = convolved + conv_weight[offset][None, :] * padded[offset : offset + tok_rows]
    activated = jax.nn.silu(convolved)
    delta = jax.nn.softplus(
        jnp.dot(dt_low, dt_weight, preferred_element_type=jnp.float32) + dt_bias[None, :]
    )
    rates = -jnp.exp(a_log)
    b_rows = b_and_c[0].T
    c_rows = b_and_c[1].T
    zero_state = jnp.zeros(rates.shape, jnp.float32)
    readout, weighted_all, end_state, end_product = mixer_scan(
        delta, activated, b_rows, c_rows, rates, zero_state
    )
    identity = (jnp.ones(rates.shape, jnp.float32), jnp.zeros(rates.shape, jnp.float32))
    carried = carried_in((end_product, end_state), "seq", link_pairs, identity)
    entering = carried[1]
    readout = mixer_scan(delta, activated, b_rows, c_rows, rates, entering)[0]
    mamba_out = (
        (readout + d_skip[None, :] * activated) * jax.nn.silu(z_gate.astype(jnp.float32))
    ).astype(jnp.bfloat16)
    experts = router.shape[1]
    picks = expert_ids.shape[1]
    feature_width = hidden.shape[1]
    group_size = lax.axis_size("seq") // experts
    logits = lax.psum(jnp.dot(hidden, router, preferred_element_type=jnp.float32), "exp")
    expert_iota = lax.broadcasted_iota(jnp.int32, (1, 1, experts), 2)
    chosen = expert_ids[:, :, None] == expert_iota
    picked = jnp.sum(jnp.where(chosen, logits[:, None, :], 0.0), axis=2)
    gates = jax.nn.sigmoid(picked - picked[:, ::-1])
    flat_hits = chosen.reshape(tok_rows * picks, experts).astype(jnp.int32)
    earlier_hits = jnp.cumsum(flat_hits, axis=0) - flat_hits
    slots = jnp.sum(earlier_hits * flat_hits, axis=1).reshape(tok_rows, picks)
    slot_keys = expert_ids * CAP + slots
    slot_iota = lax.broadcasted_iota(jnp.int32, (experts * CAP, 1, 1), 0)
    matches = slot_keys[None] == slot_iota
    selector = jnp.sum(matches.astype(jnp.float32), axis=2).astype(jnp.bfloat16)
    blending = jnp.sum(jnp.where(matches, gates[None], 0.0), axis=2)
    packed = jnp.dot(selector, hidden, preferred_element_type=jnp.float32).astype(jnp.bfloat16)
    outgoing = jnp.broadcast_to(
        packed.reshape(experts, 1, CAP, feature_width), (experts, group_size, CAP, feature_width)
    )
    outgoing = outgoing.reshape(experts * group_size, CAP, feature_width)
    arrived = lax.all_to_all(outgoing, "seq", split_axis=0, concat_axis=0, tiled=True)
    sources, entries, features = arrived.shape
    routed = arrived.reshape(sources * entries, features)
    partial_value = jnp.dot(routed, w_gate, preferred_element_type=jnp.float32)
    summed = lax.psum(partial_value.astype(jnp.bfloat16), "exp").astype(jnp.float32)
    acted = jax.nn.silu(summed).astype(jnp.bfloat16)
    produced = jnp.dot(acted, w_down, preferred_element_type=jnp.float32)
    produced = produced.reshape(sources, entries, features)
    returned = lax.all_to_all(
        produced.astype(jnp.bfloat16), "seq", split_axis=0, concat_axis=0, tiled=True
    ).astype(produced.dtype)
    combined = jnp.sum(returned.reshape(experts, group_size, CAP, feature_width), axis=1).reshape(
        experts * CAP, feature_width
    )
    moe_out = jnp.einsum("rt,rd->td", blending, combined, precision=lax.Precision.HIGHEST)
    return (mamba_out, moe_out.astype(jnp.bfloat16))


def solution(mesh):
    return jax.shard_map(
        local,
        mesh=mesh,
        in_specs=(
            P("seq", "exp"),
            P("seq", "exp"),
            P("seq", None),
            P(None, "exp"),
            P("exp"),
            P(None, "exp"),
            P(None, "exp"),
            P("exp"),
            P("exp"),
            P(None, None, "seq"),
            P("seq", "exp"),
            P("exp", None),
            P("seq", None),
            P("exp", "seq"),
            P("seq", "exp"),
        ),
        out_specs=(P("seq", "exp"), P("seq", "exp")),
        check_vma=False,
    )
```

profile of v0, /device:TPU:2, one launch (start us, length us, event | category | flops | bytes accessed | tf_op | source)
XLA Modules:
  0.0 475.2 jit_solution(18132872191936348174)
XLA Ops:
  8.9 3.5 collective-permute-start
  14.1 1.4 compare_select_fusion
  15.5 1.3 slice_bitcast_fusion
  16.9 0.9 maximum_convert_fusion
  18.7 4.2 while.39
  23.9 12.6 %psum.14 = f32[64,8]{0,1:T(8,128)S(1)} all-reduce(f32[64,8]{0,1:T(8,128)S(1)} %fusion.109), channel_id=1, replica_groups=mesh['seq'=64,'exp'=8] {'exp'}, use_global_device_ids=true, to_apply=%region_24.25 | all-reduce | flops 512 | bytes 4096 | tf_op jit(solution)/shard_map/psum | solution.py:116
  38.4 1.3 broadcast_in_dim.47
  39.7 17.2 %all-to-all-start = ((bf16[64,18,512]{2,1,0:T(8,128)(2,1)}), bf16[64,18,512]{2,1,0:T(8,128)(2,1)S(1)}, u32[]{:S(2)}, u32[]{:S(2)}) async-start(bf16[64,18,512]{2,1,0:T(8,128)(2,1)} %bitcast.98), calls=%async_computation | async-start | bytes 3145728 | tf_op jit(solution)/shard_map/all_to_all | solution.py:134
  56.9 1.4 convert_element_type.62
  58.5 75.3 %all-to-all-done = bf16[64,18,512]{2,1,0:T(8,128)(2,1)S(1)} async-done(((bf16[64,18,512]{2,1,0:T(8,128)(2,1)}), bf16[64,18,512]{2,1,0:T(8,128)(2,1)S(1)}, u32[]{:S(2)}, u32[]{:S(2)}) %all-to-all-start) | async-done | bytes 1179680 | tf_op jit(solution)/shard_map/all_to_all | solution.py:134
  133.7 1.2 reshape.657
  134.9 5.0 %convolution_convert_fusion = bf16[1152,1536]{1,0:T(8,128)(2,1)} fusion(bf16[1152,512]{1,0:T(8,128)(2,1)} %reshape.657, bf16[512,1536]{1,0:T(8,128)(2,1)S(1)} %copy-done), kind=kOutput, calls=%fused_computation.255 | convolution fusion | flops 1813708800 | bytes 6291456 | tf_op jit(solution)/shard_map/dot_general | solution.py:137
  140.8 52.6 %all-gather.5.cloned.1.call-done = bf16[1024,1024]{1,0:T(8,128)(2,1)} async-done(((bf16[16,1024]{1,0:T(8,128)(2,1)}), bf16[1024,1024]{1,0:T(8,128)(2,1)}) %all-gather.5.cloned.1.call-update) | async-done | bytes 2097168 | tf_op jit(solution)/shard_map/all_gather | solution.py:18
  193.4 140.1 %all-gather.7.cloned.1.call-done = bf16[1024,1024]{1,0:T(8,128)(2,1)} async-done(((bf16[16,1024]{1,0:T(8,128)(2,1)}), bf16[1024,1024]{1,0:T(8,128)(2,1)}) %all-gather.7.cloned.1.call-update) | async-done | bytes 2097168 | tf_op jit(solution)/shard_map/all_gather | solution.py:18
  333.5 4.6 fusion.93
  338.1 1.3 convert_element_type.73
  339.4 57.4 %all-to-all-start.1 = ((bf16[64,18,512]{2,1,0:T(8,128)(2,1)}), bf16[64,18,512]{2,1,0:T(8,128)(2,1)}, u32[]{:S(2)}, u32[]{:S(2)}) async-start(bf16[64,18,512]{2,1,0:T(8,128)(2,1)} %convert_element_type.73), calls=%async_computation.1 | async-start | bytes 3145728 | tf_op jit(solution)/shard_map/all_to_all | solution.py:142
  396.8 12.9 %while.38 = (s32[]{:T(128)}, f32[16,1024]{1,0:T(8,128)S(1)}, f32[4,16,1024]{2,1,0:T(8,128)S(1)}, f32[4,16,1024]{2,1,0:T(8,128)}, f32[16,1024]{1,0:T(8,128)S(1)},...) while((s32[]{:T(128)}, f32[16,1024]{1,0:T(8,128)S(1)}, ...), condition=%wide.region_21.22_spmd, body=%wide.region_4.21_spmd.sunk | while | flops 2359313 | bytes 1940765 | solution.py:62
  397.0 1.8 constant_dynamic-slice_fusion.114
  400.2 1.8 constant_dynamic-slice_fusion.114
  403.5 1.8 constant_dynamic-slice_fusion.114
  406.7 1.8 constant_dynamic-slice_fusion.114
  410.7 54.4 %all-to-all-done.1 = bf16[64,18,512]{2,1,0:T(8,128)(2,1)} async-done(((bf16[64,18,512]{2,1,0:T(8,128)(2,1)}), bf16[64,18,512]{2,1,0:T(8,128)(2,1)}, u32[]{:S(2)}, u32[]{:S(2)}) %all-to-all-start.1) | async-done | bytes 1179680 | tf_op jit(solution)/shard_map/all_to_all | solution.py:142
  465.1 1.7 convert_reduce_fusion
  (238 shorter events, 17.7 us)
Async XLA Ops:
  8.0 126.9 %copy-start = (bf16[512,1536]{1,0:T(8,128)(2,1)S(1)}, bf16[512,1536]{1,0:T(8,128)(2,1)}, u32[]{:S(2)}) copy-start(bf16[512,1536]{1,0:T(8,128)(2,1)} %param.34) | copy-start | bytes 4718596
  8.0 185.4 %all-gather.5.cloned.1.call-start = ((), (), s32[]{:S(2)}) async-start(), calls=%async_computation.3 | async-start | bytes 2129920 | tf_op jit(solution)/shard_map/all_gather | solution.py:18
  8.9 8.0 %collective-permute-start = (bf16[3,1024]{1,0:T(4,128)(2,1)S(1)}, bf16[3,1024]{1,0:T(4,128)(2,1)S(1)}, u32[]{:S(2)}, u32[]{:S(2)}) collective-permute-start(bf16[3,1024]{1,0:T(4,128)(2,1)S(1)} %slice.515), channel_id=1, source_target_pairs={{0,8},{8,16},{16,24},{24,32},{32,40},{40,48},{48,56},{56,64},{64,7... | collective-permute-start | bytes 18440 | tf_op jit(solution)/shard_map/ppermute | solution.py:12
  18.7 5.0 %copy-start.9 = (s32[64,2]{0,1:T(2,128)S(1)}, s32[64,2]{0,1:T(2,128)}, u32[]{:S(2)}) copy-start(s32[64,2]{0,1:T(2,128)} %param.33) | copy-start | bytes 1540
  18.7 5.1 %copy-start.3 = (bf16[64,512]{1,0:T(8,128)(2,1)S(1)}, bf16[64,512]{1,0:T(8,128)(2,1)}, u32[]{:S(2)}) copy-start(bf16[64,512]{1,0:T(8,128)(2,1)} %param.31) | copy-start | bytes 196612
  18.7 5.0 %copy-start.10 = (bf16[512,8]{0,1:T(8,128)(2,1)S(1)}, bf16[512,8]{0,1:T(8,128)(2,1)}, u32[]{:S(2)}) copy-start(bf16[512,8]{0,1:T(8,128)(2,1)} %param.32) | copy-start | bytes 24580
  22.9 13.7 %copy-start.6 = (f32[16,1024]{1,0:T(8,128)}, f32[16,1024]{1,0:T(8,128)S(1)}, u32[]{:S(2)}) copy-start(f32[16,1024]{1,0:T(8,128)S(1)} %get-tuple-element.127) | copy-start | bytes 196612
  22.9 16.8 %copy-start.1 = (f32[4,16,1024]{2,1,0:T(8,128)}, f32[4,16,1024]{2,1,0:T(8,128)S(1)}, u32[]{:S(2)}) copy-start(f32[4,16,1024]{2,1,0:T(8,128)S(1)} %get-tuple-element.950) | copy-start | bytes 786436
  22.9 16.7 %copy-start.2 = (f32[4,16,1024]{2,1,0:T(8,128)}, f32[4,16,1024]{2,1,0:T(8,128)S(1)}, u32[]{:S(2)}) copy-start(f32[4,16,1024]{2,1,0:T(8,128)S(1)} %get-tuple-element.951) | copy-start | bytes 786436
  39.7 94.1 %all-to-all-start = ((bf16[64,18,512]{2,1,0:T(8,128)(2,1)}), bf16[64,18,512]{2,1,0:T(8,128)(2,1)S(1)}, u32[]{:S(2)}, u32[]{:S(2)}) async-start(bf16[64,18,512]{2,1,0:T(8,128)(2,1)} %bitcast.98), calls=%async_computation | async-start | bytes 3145728 | tf_op jit(solution)/shard_map/all_to_all | solution.py:134
  56.9 276.6 %all-gather.7.cloned.1.call-start = ((), (), s32[]{:S(2)}) async-start(), calls=%async_computation.4 | async-start | bytes 2129920 | tf_op jit(solution)/shard_map/all_gather | solution.py:18
  58.4 275.1 %all-reduce.2.cloned.1.call-start = ((), (), s32[]{:S(2)}) async-start(), calls=%async_computation.2 | async-start | bytes 7077888 | tf_op jit(solution)/shard_map/psum | solution.py:138
  140.0 0.7 copy-start.7
  339.4 125.7 %all-to-all-start.1 = ((bf16[64,18,512]{2,1,0:T(8,128)(2,1)}), bf16[64,18,512]{2,1,0:T(8,128)(2,1)}, u32[]{:S(2)}, u32[]{:S(2)}) async-start(bf16[64,18,512]{2,1,0:T(8,128)(2,1)} %convert_element_type.73), calls=%async_computation.1 | async-start | bytes 3145728 | tf_op jit(solution)/shard_map/all_to_all | solution.py:142
  396.8 13.0 %copy-start.5 = (bf16[64,1024]{1,0:T(8,128)(2,1)S(1)}, bf16[64,1024]{1,0:T(8,128)(2,1)}, u32[]{:S(2)}) copy-start(bf16[64,1024]{1,0:T(8,128)(2,1)} %param.22) | copy-start | bytes 393220
  396.8 13.0 %copy-start.8 = (f32[1024]{0:T(1024)S(1)}, f32[1024]{0:T(1024)}, u32[]{:S(2)}) copy-start(f32[1024]{0:T(1024)} %param.28) | copy-start | bytes 12292
  396.8 13.0 %copy-start.11 = (f32[1024]{0:T(1024)S(1)}, f32[1024]{0:T(1024)}, u32[]{:S(2)}) copy-start(f32[1024]{0:T(1024)} %param.29) | copy-start | bytes 12292
  409.8 57.1 %copy-start.4 = (f32[144,64]{0,1:T(8,128)S(1)}, f32[144,64]{0,1:T(8,128)}, u32[]{:S(2)}) copy-start(f32[144,64]{0,1:T(8,128)} %get-tuple-element.170) | copy-start | bytes 110596
Sparse Core Ops, SparseCore 0:
  23.8 169.5 all-gather.4
  196.3 137.1 all-gather.6
Sparse Core Ops, SparseCore 1:
  140.1 77.3 all-reduce.1
where the time goes:
time: 481 us; the launch traced here: 475 us
  waiting for transfers between devices  322 us (67%)
  starting transfers between devices  78.2 us (16%)
  local copies, waits for them, and re-layouts  18 us (4%)
  between operations  15.8 us (3%)
  other arithmetic  14.6 us (3%)
  blocking collectives  12.6 us (3%)
  matrix products  12.2 us (3%)
    all_gather x2, waiting for transfers between devices, carried_in(): lax.all_gather(a.astype(kind), axis)  193 us
    all_to_all x1, waiting for transfers between devices, local(): lax.all_to_all(outgoing, 'seq', split_axis=0, concat_axis=0, tiled=True)  75.3 us
    all_to_all x1, starting transfers between devices, local(): lax.all_to_all(produced.astype(jnp.bfloat16), 'seq', split_axis=0, concat...  57.4 us
    all_to_all x1, waiting for transfers between devices, local(): lax.all_to_all(produced.astype(jnp.bfloat16), 'seq', split_axis=0, concat...  54.4 us
    all_to_all x1, starting transfers between devices, local(): lax.all_to_all(outgoing, 'seq', split_axis=0, concat_axis=0, tiled=True)  17.2 us
    psum x1, blocking collectives, local(): lax.psum(jnp.dot(hidden, router, preferred_element_type=jnp.float32), 'exp')  12.6 us
  transfers between devices with their start and end apart: 6, of which 4 were waited for; matrix products, arithmetic and copies ran while one was open for 6% of the time, Pallas kernels for 0%

commit v1 on v0

--- a/solution.py
+++ b/solution.py
@@ -113,7 +113,9 @@
     picks = expert_ids.shape[1]
     feature_width = hidden.shape[1]
     group_size = lax.axis_size("seq") // experts
-    logits = lax.psum(jnp.dot(hidden, router, preferred_element_type=jnp.float32), "exp")
+    logits = jnp.sum(
+        lax.all_gather(jnp.dot(hidden, router, preferred_element_type=jnp.float32), "exp"), axis=0
+    )
     expert_iota = lax.broadcasted_iota(jnp.int32, (1, 1, experts), 2)
     chosen = expert_ids[:, :, None] == expert_iota
     picked = jnp.sum(jnp.where(chosen, logits[:, None, :], 0.0), axis=2)

time: 481 us -> 465 us (0.967)
  waiting for transfers between devices: 322 us -> 305 us
    all_gather x2, waiting for transfers between devices: 193 us -> 173 us  [carried_in(): lax.all_gather(a.astype(kind), axis)]
    all_gather x0 -> x1, blocking collectives: none -> 13.5 us  [local(): lax.all_gather(jnp.dot(hidden, router, preferred_element_type=jnp.float32...]
    psum x1 -> x0, blocking collectives: 12.6 us -> none  [local(): lax.psum(jnp.dot(hidden, router, preferred_element_type=jnp.float32), 'exp')]
where the time goes in v1:
time: 465 us; the launch traced here: 460 us
  waiting for transfers between devices  305 us (66%)
  starting transfers between devices  78.9 us (17%)
  local copies, waits for them, and re-layouts  18 us (4%)
  between operations  15.8 us (3%)
  other arithmetic  14.6 us (3%)
  blocking collectives  13.5 us (3%)
  matrix products  12.2 us (3%)
    all_gather x2, waiting for transfers between devices, carried_in(): lax.all_gather(a.astype(kind), axis)  173 us
    all_to_all x1, waiting for transfers between devices, local(): lax.all_to_all(outgoing, 'seq', split_axis=0, concat_axis=0, tiled=True)  78.5 us
    all_to_all x1, starting transfers between devices, local(): lax.all_to_all(produced.astype(jnp.bfloat16), 'seq', split_axis=0, concat...  57.4 us
    all_to_all x1, waiting for transfers between devices, local(): lax.all_to_all(produced.astype(jnp.bfloat16), 'seq', split_axis=0, concat...  54.4 us
    all_to_all x1, starting transfers between devices, local(): lax.all_to_all(outgoing, 'seq', split_axis=0, concat_axis=0, tiled=True)  17.9 us
    all_gather x1, blocking collectives, local(): lax.all_gather(jnp.dot(hidden, router, preferred_element_type=jnp.float32...  13.5 us
  transfers between devices with their start and end apart: 6, of which 4 were waited for; matrix products, arithmetic and copies ran while one was open for 6% of the time, Pallas kernels for 0%

profile of v1, /device:TPU:2, one launch (start us, length us, event | category | flops | bytes accessed | tf_op | source)
XLA Modules:
  0.0 459.7 jit_solution(12764481120808743134)
XLA Ops:
  8.9 3.5 collective-permute-start
  14.1 1.4 compare_select_fusion
  15.5 1.3 slice_bitcast_fusion
  16.9 0.9 maximum_convert_fusion
  18.7 4.2 while.39
  23.9 13.5 %all-gather.3 = f32[8,64,8]{1,2,0:T(8,128)S(1)} all-gather(f32[1,64,8]{1,2,0:T(8,128)S(1)} %convolution_bitcast_fusion), channel_id=4, replica_groups=mesh['seq'=64,'exp'=8] {'exp'}, dimensions={0}, use_global_device_ids=true | all-gather | bytes 18432 | tf_op jit(solution)/shard_map/all_gather | solution.py:117
  39.2 1.3 broadcast_in_dim.47
  40.5 17.9 %all-to-all-start = ((bf16[64,18,512]{2,1,0:T(8,128)(2,1)}), bf16[64,18,512]{2,1,0:T(8,128)(2,1)S(1)}, u32[]{:S(2)}, u32[]{:S(2)}) async-start(bf16[64,18,512]{2,1,0:T(8,128)(2,1)} %bitcast.99), calls=%async_computation | async-start | bytes 3145728 | tf_op jit(solution)/shard_map/all_to_all | solution.py:136
  58.5 1.4 convert_element_type.62
  60.0 78.5 %all-to-all-done = bf16[64,18,512]{2,1,0:T(8,128)(2,1)S(1)} async-done(((bf16[64,18,512]{2,1,0:T(8,128)(2,1)}), bf16[64,18,512]{2,1,0:T(8,128)(2,1)S(1)}, u32[]{:S(2)}, u32[]{:S(2)}) %all-to-all-start) | async-done | bytes 1179680 | tf_op jit(solution)/shard_map/all_to_all | solution.py:136
  138.5 1.2 reshape.657
  139.6 5.0 %convolution_convert_fusion = bf16[1152,1536]{1,0:T(8,128)(2,1)} fusion(bf16[1152,512]{1,0:T(8,128)(2,1)} %reshape.657, bf16[512,1536]{1,0:T(8,128)(2,1)S(1)} %copy-done), kind=kOutput, calls=%fused_computation.255 | convolution fusion | flops 1813708800 | bytes 6291456 | tf_op jit(solution)/shard_map/dot_general | solution.py:139
  145.5 31.4 %all-gather.7.cloned.1.call-done = bf16[1024,1024]{1,0:T(8,128)(2,1)} async-done(((bf16[16,1024]{1,0:T(8,128)(2,1)}), bf16[1024,1024]{1,0:T(8,128)(2,1)}) %all-gather.7.cloned.1.call-update) | async-done | bytes 2097168 | tf_op jit(solution)/shard_map/all_gather | solution.py:18
  176.9 141.1 %all-gather.9.cloned.1.call-done = bf16[1024,1024]{1,0:T(8,128)(2,1)} async-done(((bf16[16,1024]{1,0:T(8,128)(2,1)}), bf16[1024,1024]{1,0:T(8,128)(2,1)}) %all-gather.9.cloned.1.call-update) | async-done | bytes 2097168 | tf_op jit(solution)/shard_map/all_gather | solution.py:18
  318.0 4.5 fusion.93
  322.5 1.3 convert_element_type.73
  323.9 57.4 %all-to-all-start.1 = ((bf16[64,18,512]{2,1,0:T(8,128)(2,1)}), bf16[64,18,512]{2,1,0:T(8,128)(2,1)}, u32[]{:S(2)}, u32[]{:S(2)}) async-start(bf16[64,18,512]{2,1,0:T(8,128)(2,1)} %convert_element_type.73), calls=%async_computation.1 | async-start | bytes 3145728 | tf_op jit(solution)/shard_map/all_to_all | solution.py:144
  381.3 12.9 %while.38 = (s32[]{:T(128)}, f32[16,1024]{1,0:T(8,128)S(1)}, f32[4,16,1024]{2,1,0:T(8,128)S(1)}, f32[4,16,1024]{2,1,0:T(8,128)}, f32[16,1024]{1,0:T(8,128)S(1)},...) while((s32[]{:T(128)}, f32[16,1024]{1,0:T(8,128)S(1)}, ...), condition=%wide.region_21.22_spmd, body=%wide.region_4.21_spmd.sunk | while | flops 2359313 | bytes 1940765 | solution.py:62
  381.5 1.8 constant_dynamic-slice_fusion.114
  384.7 1.8 constant_dynamic-slice_fusion.114
  388.0 1.8 constant_dynamic-slice_fusion.114
  391.2 1.8 constant_dynamic-slice_fusion.114
  395.2 54.4 %all-to-all-done.1 = bf16[64,18,512]{2,1,0:T(8,128)(2,1)} async-done(((bf16[64,18,512]{2,1,0:T(8,128)(2,1)}), bf16[64,18,512]{2,1,0:T(8,128)(2,1)}, u32[]{:S(2)}, u32[]{:S(2)}) %all-to-all-start.1) | async-done | bytes 1179680 | tf_op jit(solution)/shard_map/all_to_all | solution.py:144
  449.6 1.7 convert_reduce_fusion
  (239 shorter events, 17.7 us)
Async XLA Ops:
  8.0 131.7 %copy-start = (bf16[512,1536]{1,0:T(8,128)(2,1)S(1)}, bf16[512,1536]{1,0:T(8,128)(2,1)}, u32[]{:S(2)}) copy-start(bf16[512,1536]{1,0:T(8,128)(2,1)} %param.34) | copy-start | bytes 4718596
  8.0 168.9 %all-gather.7.cloned.1.call-start = ((), (), s32[]{:S(2)}) async-start(), calls=%async_computation.3 | async-start | bytes 2129920 | tf_op jit(solution)/shard_map/all_gather | solution.py:18
  8.9 8.0 %collective-permute-start = (bf16[3,1024]{1,0:T(4,128)(2,1)S(1)}, bf16[3,1024]{1,0:T(4,128)(2,1)S(1)}, u32[]{:S(2)}, u32[]{:S(2)}) collective-permute-start(bf16[3,1024]{1,0:T(4,128)(2,1)S(1)} %slice.515), channel_id=1, source_target_pairs={{0,8},{8,16},{16,24},{24,32},{32,40},{40,48},{48,56},{56,64},{64,7... | collective-permute-start | bytes 18440 | tf_op jit(solution)/shard_map/ppermute | solution.py:12
  18.7 5.0 %copy-start.9 = (s32[64,2]{0,1:T(2,128)S(1)}, s32[64,2]{0,1:T(2,128)}, u32[]{:S(2)}) copy-start(s32[64,2]{0,1:T(2,128)} %param.33) | copy-start | bytes 1540
  18.7 5.1 %copy-start.3 = (bf16[64,512]{1,0:T(8,128)(2,1)S(1)}, bf16[64,512]{1,0:T(8,128)(2,1)}, u32[]{:S(2)}) copy-start(bf16[64,512]{1,0:T(8,128)(2,1)} %param.31) | copy-start | bytes 196612
  18.7 5.0 %copy-start.10 = (bf16[512,8]{0,1:T(8,128)(2,1)S(1)}, bf16[512,8]{0,1:T(8,128)(2,1)}, u32[]{:S(2)}) copy-start(bf16[512,8]{0,1:T(8,128)(2,1)} %param.32) | copy-start | bytes 24580
  22.9 14.5 %copy-start.6 = (f32[16,1024]{1,0:T(8,128)}, f32[16,1024]{1,0:T(8,128)S(1)}, u32[]{:S(2)}) copy-start(f32[16,1024]{1,0:T(8,128)S(1)} %get-tuple-element.127) | copy-start | bytes 196612
  22.9 17.6 %copy-start.1 = (f32[4,16,1024]{2,1,0:T(8,128)}, f32[4,16,1024]{2,1,0:T(8,128)S(1)}, u32[]{:S(2)}) copy-start(f32[4,16,1024]{2,1,0:T(8,128)S(1)} %get-tuple-element.950) | copy-start | bytes 786436
  22.9 17.6 %copy-start.2 = (f32[4,16,1024]{2,1,0:T(8,128)}, f32[4,16,1024]{2,1,0:T(8,128)S(1)}, u32[]{:S(2)}) copy-start(f32[4,16,1024]{2,1,0:T(8,128)S(1)} %get-tuple-element.951) | copy-start | bytes 786436
  40.5 97.9 %all-to-all-start = ((bf16[64,18,512]{2,1,0:T(8,128)(2,1)}), bf16[64,18,512]{2,1,0:T(8,128)(2,1)S(1)}, u32[]{:S(2)}, u32[]{:S(2)}) async-start(bf16[64,18,512]{2,1,0:T(8,128)(2,1)} %bitcast.99), calls=%async_computation | async-start | bytes 3145728 | tf_op jit(solution)/shard_map/all_to_all | solution.py:136
  58.4 259.5 %all-gather.9.cloned.1.call-start = ((), (), s32[]{:S(2)}) async-start(), calls=%async_computation.4 | async-start | bytes 2129920 | tf_op jit(solution)/shard_map/all_gather | solution.py:18
  60.0 258.0 %all-reduce.2.cloned.1.call-start = ((), (), s32[]{:S(2)}) async-start(), calls=%async_computation.2 | async-start | bytes 7077888 | tf_op jit(solution)/shard_map/psum | solution.py:140
  144.7 0.7 copy-start.7
  323.9 125.7 %all-to-all-start.1 = ((bf16[64,18,512]{2,1,0:T(8,128)(2,1)}), bf16[64,18,512]{2,1,0:T(8,128)(2,1)}, u32[]{:S(2)}, u32[]{:S(2)}) async-start(bf16[64,18,512]{2,1,0:T(8,128)(2,1)} %convert_element_type.73), calls=%async_computation.1 | async-start | bytes 3145728 | tf_op jit(solution)/shard_map/all_to_all | solution.py:144
  381.3 13.0 %copy-start.5 = (bf16[64,1024]{1,0:T(8,128)(2,1)S(1)}, bf16[64,1024]{1,0:T(8,128)(2,1)}, u32[]{:S(2)}) copy-start(bf16[64,1024]{1,0:T(8,128)(2,1)} %param.22) | copy-start | bytes 393220
  381.3 13.0 %copy-start.8 = (f32[1024]{0:T(1024)S(1)}, f32[1024]{0:T(1024)}, u32[]{:S(2)}) copy-start(f32[1024]{0:T(1024)} %param.28) | copy-start | bytes 12292
  381.3 13.0 %copy-start.11 = (f32[1024]{0:T(1024)S(1)}, f32[1024]{0:T(1024)}, u32[]{:S(2)}) copy-start(f32[1024]{0:T(1024)} %param.29) | copy-start | bytes 12292
  394.3 57.1 %copy-start.4 = (f32[144,64]{0,1:T(8,128)S(1)}, f32[144,64]{0,1:T(8,128)}, u32[]{:S(2)}) copy-start(f32[144,64]{0,1:T(8,128)} %get-tuple-element.170) | copy-start | bytes 110596
Sparse Core Ops, SparseCore 0:
  23.8 153.0 all-gather.6
  179.8 138.0 all-gather.8
Sparse Core Ops, SparseCore 1:
  144.8 75.7 all-reduce.1
